TPU v7x, 32 devices: a whole 2x2x4 slice. The times are simulated.
32 devices in a mesh: grp: 4 (over z), row: 8 (over y, x, core).
Axes of the slice: x: 2, y: 2, z: 4, core: 2. Of those that a mesh axis runs over, the one named last changes fastest.
Arguments:
- basis: float32 [8192, 1024], P(('grp', 'row')), may hold values from -40 to 40
- block: float32 [8192, 512], P(('grp', 'row')), may hold values from -600 to 600
- counts: int32 [4, 8], P('grp', 'row'), may hold values from 128 to 256, as said below
Outputs:
- new_block: float32 [8192, 512], P(('grp', 'row'))
- factor: float32 [512, 512], replicated
Inputs may be any that keep to these rules, and one draw needn't show every extreme that they name: `counts`: each device's live rows are a multiple of 128, at most 256; one device holds exactly 256.
All inputs are finite; a program needn't handle non-finite values.
Results may differ from a plain program's by a relative error of at most 0.0003.
Values sent between devices are 32-bit elements; how exact they have to be, the bound alone decides.
A program may use at most 64 MiB of HBM per device.

v0:
```python
import jax
import jax.numpy as jnp
from jax import lax
from jax.sharding import PartitionSpec as P


def transposed_product(left, right):
    return lax.dot_general(
        left,
        right,
        (((0,), (0,)), ((), ())),
        precision=lax.Precision.HIGHEST,
        preferred_element_type=jnp.float32,
    )


def matrix_product(left, right):
    return jnp.dot(left, right, precision=lax.Precision.HIGHEST, preferred_element_type=jnp.float32)


def body(basis, block, counts):
    row_slots = block.shape[0]
    devices = lax.axis_size("grp") * lax.axis_size("row")
    weight = 1.0 / (row_slots * devices)
    live = (lax.iota(jnp.int32, row_slots) < counts[0, 0]).astype(jnp.float32)[:, None]
    basis_live = basis * live
    block_live = block * live
    local_coeffs = transposed_product(basis_live, block_live) * weight
    local_metric = transposed_product(basis_live, basis_live) * weight
    coeffs, metric = lax.psum((local_coeffs, local_metric), ("grp", "row"))
    correction = coeffs - matrix_product(metric, coeffs)
    residual = block_live - matrix_product(basis_live, coeffs + correction)
    local_gram = transposed_product(residual, residual) * weight
    gram = lax.psum(local_gram, ("grp", "row"))
    lower_factor = jnp.linalg.cholesky(gram)
    new_block = lax.linalg.triangular_solve(
        lower_factor, residual, left_side=False, lower=True, transpose_a=True
    )
    return (new_block, lower_factor.T)


def solution(mesh):
    placed = (P(("grp", "row"), None), P(("grp", "row"), None), P("grp", "row"))
    return jax.shard_map(
        body, mesh=mesh, in_specs=placed, out_specs=(P(("grp", "row"), None), P()), check_vma=False
    )
```

profile of v0, /device:TPU:0, one launch (start us, length us, event | category | flops | bytes accessed | tf_op | source)
XLA Modules:
  0.0 480.0 jit_solution(1416516150197127453)
XLA Ops:
  7.9 7.3 %convolution_multiply_fusion = f32[1024,1024]{1,0:T(8,128)} fusion(f32[256,1024]{1,0:T(8,128)} %param.3, f32[256]{0:T(256)S(1)} %compare_convert_fusion), kind=kOutput, calls=%fused_computation.3 | convolution fusion | flops 3222536192 | bytes 5243904 | tf_op jit(solution)/shard_map/dot_general | solution.py:8
  15.2 3.3 convolution_multiply_fusion.1
  18.6 158.9 %all-reduce.7.cloned.1.call-done = (f32[1024,512]{1,0:T(8,128)}, f32[1024,1024]{1,0:T(8,128)}) async-done(((f32[1024,512]{1,0:T(8,128)}, f32[1024,1024]{1,0:T(8,128)}), (f32[1024,512]{1,0:T(8,128)}, f32[1024,1024]{1,0:T(8,128)})) %all-reduce.7.cloned.1.call-update) | async-done | bytes 6291472 | tf_op jit(solution)/shard_map/psum | solution.py:30
  177.5 10.1 %fusion.43 = f32[1024,512]{1,0:T(8,128)S(1)} fusion(f32[1024,1024]{1,0:T(8,128)} %get-tuple-element.21, f32[1024,512]{1,0:T(8,128)} %get-tuple-element.20), kind=kOutput, calls=%fused_computation.84 | convolution fusion | flops 6442450944 | bytes 8388608 | tf_op jit(solution)/shard_map/dot_general | solution.py:18
  187.6 2.1 fusion.1
  189.7 2.0 convolution_multiply_fusion.2
  191.8 130.8 %all-reduce.5.cloned.1.call-done = f32[512,512]{0,1:T(8,128)} async-done(((f32[512,512]{0,1:T(8,128)}), f32[512,512]{0,1:T(8,128)}) %all-reduce.5.cloned.1.call-update) | async-done | bytes 1048592 | tf_op jit(solution)/shard_map/psum | solution.py:34
  322.6 1.6 copy.6
  325.5 11.7 %cholesky.104 = f32[128,128]{1,0:T(8,128)S(1)} custom-call(f32[128,128]{1,0:T(8,128)S(1)} %cholesky.266), custom_call_target="Cholesky" | custom-call | tf_op jit(solution)/shard_map/jit(cholesky)/cholesky | solution.py:35
  337.2 9.8 %custom-call.30 = f32[1,128,128]{1,2,0:T(8,128)S(1)} custom-call(f32[1,128,128]{2,1,0:T(8,128)S(1)} %get-tuple-element.35), custom_call_target="InvertDiagBlocksLowerTriangular" | custom-call | tf_op jit(solution)/shard_map/jit(cholesky)/cholesky | solution.py:35
  349.7 11.9 %cholesky.217 = f32[128,128]{1,0:T(8,128)S(1)} custom-call(f32[128,128]{1,0:T(8,128)S(1)} %cholesky.270), custom_call_target="Cholesky" | custom-call | tf_op jit(solution)/shard_map/jit(cholesky)/cholesky | solution.py:35
  361.6 9.8 %custom-call.31 = f32[1,128,128]{1,2,0:T(8,128)S(1)} custom-call(f32[1,128,128]{2,1,0:T(8,128)S(1)} %get-tuple-element.32), custom_call_target="InvertDiagBlocksLowerTriangular" | custom-call | tf_op jit(solution)/shard_map/jit(cholesky)/cholesky | solution.py:35
  373.0 11.7 %cholesky.238 = f32[128,128]{1,0:T(8,128)S(1)} custom-call(f32[128,128]{1,0:T(8,128)S(1)} %cholesky.275), custom_call_target="Cholesky" | custom-call | tf_op jit(solution)/shard_map/jit(cholesky)/cholesky | solution.py:35
  385.5 9.8 %custom-call.32 = f32[1,128,128]{1,2,0:T(8,128)S(1)} custom-call(f32[1,128,128]{2,1,0:T(8,128)S(1)} %get-tuple-element.29), custom_call_target="InvertDiagBlocksLowerTriangular" | custom-call | tf_op jit(solution)/shard_map/jit(cholesky)/cholesky | solution.py:35
  396.7 11.9 %cholesky.255 = f32[128,128]{1,0:T(8,128)S(1)} custom-call(f32[128,128]{1,0:T(8,128)S(1)} %convolution_subtract_fusion.5), custom_call_target="Cholesky" | custom-call | tf_op jit(solution)/shard_map/jit(cholesky)/cholesky | solution.py:35
  413.7 11.7 %while.1 = (s32[]{:T(128)}, f32[512,512]{1,0:T(8,128)}, s32[4,2]{0,1:T(2,128)S(1)}, f32[4,128,128]{2,1,0:T(8,128)S(1)}, s32[]{:T(128)}) while((s32[]{:T(128)}, f32[512,512]{1,0:T(8,128)}, s32[4,2]{0,1:T(2,128)S(1)}, f32[4,128,128]{2,1,0:T(8,128)S(1)}, s32[]{:T(128)}) %tuple.33), condition=%wide.while_cond, body=%wide.while_body.sunk | while | flops 2 | bytes 131181 | solution.py:36
  414.4 2.2 bitcast_dynamic-update-slice_fusion.2
  417.3 2.2 bitcast_dynamic-update-slice_fusion.2
  420.3 2.2 bitcast_dynamic-update-slice_fusion.2
  423.2 2.2 bitcast_dynamic-update-slice_fusion.2
  425.4 39.3 %custom-call.33 = f32[4,128,128]{1,2,0:T(8,128)S(1)} custom-call(f32[4,128,128]{2,1,0:T(8,128)S(1)} %get-tuple-element.9), custom_call_target="InvertDiagBlocksLowerTriangular" | custom-call | tf_op jit(solution)/shard_map/triangular_solve | solution.py:36
  466.6 1.5 convolution_subtract_fusion.2
  468.5 1.8 convolution_subtract_fusion.1
  471.6 1.3 copy.8
  (52 shorter events, 16.6 us)
Async XLA Ops:
  7.2 170.4 %all-reduce.7.cloned.1.call-start = ((), (), s32[]{:S(2)}) async-start(), calls=%async_computation.1 | async-start | bytes 12582912 | tf_op jit(solution)/shard_map/psum | solution.py:30
  7.9 7.4 %copy-start = (f32[256,1024]{1,0:T(8,128)S(1)}, f32[256,1024]{1,0:T(8,128)}, u32[]{:S(2)}) copy-start(f32[256,1024]{1,0:T(8,128)} %param.3) | copy-start | bytes 3145732
  7.9 7.3 %copy-start.4 = (f32[256,512]{1,0:T(8,128)S(1)}, f32[256,512]{1,0:T(8,128)}, u32[]{:S(2)}) copy-start(f32[256,512]{1,0:T(8,128)} %param.4) | copy-start | bytes 1572868
  18.5 304.0 %all-reduce.5.cloned.1.call-start = ((), (), s32[]{:S(2)}) async-start(), calls=%async_computation | async-start | bytes 2097152 | tf_op jit(solution)/shard_map/psum | solution.py:34
  177.5 10.1 %copy-start.1 = (f32[1024,512]{1,0:T(8,128)S(1)}, f32[1024,512]{1,0:T(8,128)}, u32[]{:S(2)}) copy-start(f32[1024,512]{1,0:T(8,128)} %get-tuple-element.20) | copy-start | bytes 6291460
  322.6 1.7 copy-start.2
  324.5 1.0 copy-start.3
Sparse Core Ops, SparseCore 0:
  18.7 158.8 all-reduce.6
  191.9 130.6 all-reduce.4
where the time goes:
time: 487 us; the launch traced here: 480 us
  waiting for transfers between devices  290 us (60%)
  other arithmetic  120 us (25%)
  matrix products  36 us (7%)
  between operations  17.7 us (4%)
  local copies, waits for them, and re-layouts  16.7 us (3%)
    psum x1, waiting for transfers between devices, body(): coeffs, metric = lax.psum((local_coeffs, local_metric), ('grp', 'row'))  159 us
    psum x1, waiting for transfers between devices, body(): gram = lax.psum(local_gram, ('grp', 'row'))  131 us
    another operation x14, other arithmetic, body(): lower_factor = jnp.linalg.cholesky(gram)  78.8 us
    another operation x3, other arithmetic, body(): lax.linalg.triangular_solve(lower_factor, residual, left_side=False, lowe...  39.4 us
    dot_general x3, matrix products, transposed_product(): lax.dot_general(left, right, (((0,), (0,)), ((), ())), precision=lax.Prec...  12.6 us
    dot_general x2, matrix products, matrix_product(): jnp.dot(left, right, precision=lax.Precision.HIGHEST, preferred_element_t...  12.2 us
    another operation x12, local copies, waits for them, and re-layouts  11.6 us
  transfers between devices with their start and end apart: 2, of which 2 were waited for; matrix products, arithmetic and copies ran while one was open for 0% of the time, Pallas kernels for 0%

commit v1 on v0

--- a/solution.py
+++ b/solution.py
@@ -27,7 +27,7 @@
     block_live = block * live
     local_coeffs = transposed_product(basis_live, block_live) * weight
     local_metric = transposed_product(basis_live, basis_live) * weight
-    coeffs, metric = lax.psum((local_coeffs, local_metric), ("grp", "row"))
+    coeffs, metric = lax.psum(lax.psum((local_coeffs, local_metric), "grp"), "row")
     correction = coeffs - matrix_product(metric, coeffs)
     residual = block_live - matrix_product(basis_live, coeffs + correction)
     local_gram = transposed_product(residual, residual) * weight

time: 487 us -> 660 us (1.36)
  waiting for transfers between devices: 290 us -> 463 us
    psum x1 -> x2, waiting for transfers between devices: 159 us -> 332 us  [the longest x1 226 us: body(): lax.psum((local_coeffs, local_metric), 'grp')]
  transfers between devices with their start and end apart: 2 -> 3, of which waited for: 2 -> 3; matrix products, arithmetic and copies ran while one was open for 0% -> 0% of each run, Pallas kernels for 0% -> 0%
where the time goes in v1:
time: 660 us; the launch traced here: 653 us
  waiting for transfers between devices  463 us (70%)
  other arithmetic  120 us (18%)
  matrix products  36 us (5%)
  between operations  17.4 us (3%)
  local copies, waits for them, and re-layouts  16.7 us (3%)
    psum x1, waiting for transfers between devices, body(): lax.psum((local_coeffs, local_metric), 'grp')  226 us
    psum x1, waiting for transfers between devices, body(): gram = lax.psum(local_gram, ('grp', 'row'))  131 us
    psum x1, waiting for transfers between devices, body(): lax.psum(lax.psum((local_coeffs, local_metric), 'grp'), 'row')  106 us
    another operation x14, other arithmetic, body(): lower_factor = jnp.linalg.cholesky(gram)  78.8 us
    another operation x3, other arithmetic, body(): lax.linalg.triangular_solve(lower_factor, residual, left_side=False, lowe...  39.4 us
  transfers between devices with their start and end apart: 3, of which 3 were waited for; matrix products, arithmetic and copies ran while one was open for 0% of the time, Pallas kernels for 0%

profile of v1, /device:TPU:0, one launch (start us, length us, event | category | flops | bytes accessed | tf_op | source)
XLA Modules:
  0.0 652.8 jit_solution(6936539080781134987)
XLA Ops:
  7.9 7.3 %convolution_multiply_fusion = f32[1024,1024]{1,0:T(8,128)} fusion(f32[256,1024]{1,0:T(8,128)} %param.3, f32[256]{0:T(256)S(1)} %compare_convert_fusion), kind=kOutput, calls=%fused_computation.3 | convolution fusion | flops 3222536192 | bytes 5243904 | tf_op jit(solution)/shard_map/dot_general | solution.py:8
  15.2 3.3 convolution_multiply_fusion.1
  18.6 225.7 %all-reduce.11.cloned.1.call-done = (f32[1024,512]{1,0:T(8,128)}, f32[1024,1024]{1,0:T(8,128)}) async-done(((f32[1024,512]{1,0:T(8,128)}, f32[1024,1024]{1,0:T(8,128)}), (f32[1024,512]{1,0:T(8,128)}, f32[1024,1024]{1,0:T(8,128)})) %all-reduce.11.cloned.1.call-update) | async-done | bytes 6291472 | tf_op jit(solution)/shard_map/psum | solution.py:30
  244.4 106.2 %all-reduce.9.cloned.1.call-done = (f32[1024,512]{1,0:T(8,128)}, f32[1024,1024]{1,0:T(8,128)}) async-done(((f32[1024,512]{1,0:T(8,128)}, f32[1024,1024]{1,0:T(8,128)}), (f32[1024,512]{1,0:T(8,128)}, f32[1024,1024]{1,0:T(8,128)})) %all-reduce.9.cloned.1.call-update) | async-done | bytes 6291472 | tf_op jit(solution)/shard_map/psum | solution.py:30
  350.5 10.1 %fusion.43 = f32[1024,512]{1,0:T(8,128)S(1)} fusion(f32[1024,1024]{1,0:T(8,128)} %get-tuple-element.21, f32[1024,512]{1,0:T(8,128)} %get-tuple-element.20), kind=kOutput, calls=%fused_computation.84 | convolution fusion | flops 6442450944 | bytes 8388608 | tf_op jit(solution)/shard_map/dot_general | solution.py:18
  360.6 2.1 fusion.1
  362.7 2.0 convolution_multiply_fusion.2
  364.8 131.0 %all-reduce.7.cloned.1.call-done = f32[512,512]{0,1:T(8,128)} async-done(((f32[512,512]{0,1:T(8,128)}), f32[512,512]{0,1:T(8,128)}) %all-reduce.7.cloned.1.call-update) | async-done | bytes 1048592 | tf_op jit(solution)/shard_map/psum | solution.py:34
  495.8 1.6 copy.6
  498.6 11.7 %cholesky.104 = f32[128,128]{1,0:T(8,128)S(1)} custom-call(f32[128,128]{1,0:T(8,128)S(1)} %cholesky.266), custom_call_target="Cholesky" | custom-call | tf_op jit(solution)/shard_map/jit(cholesky)/cholesky | solution.py:35
  510.4 9.8 %custom-call.30 = f32[1,128,128]{1,2,0:T(8,128)S(1)} custom-call(f32[1,128,128]{2,1,0:T(8,128)S(1)} %get-tuple-element.37), custom_call_target="InvertDiagBlocksLowerTriangular" | custom-call | tf_op jit(solution)/shard_map/jit(cholesky)/cholesky | solution.py:35
  522.9 11.9 %cholesky.217 = f32[128,128]{1,0:T(8,128)S(1)} custom-call(f32[128,128]{1,0:T(8,128)S(1)} %cholesky.270), custom_call_target="Cholesky" | custom-call | tf_op jit(solution)/shard_map/jit(cholesky)/cholesky | solution.py:35
  534.8 9.8 %custom-call.31 = f32[1,128,128]{1,2,0:T(8,128)S(1)} custom-call(f32[1,128,128]{2,1,0:T(8,128)S(1)} %get-tuple-element.34), custom_call_target="InvertDiagBlocksLowerTriangular" | custom-call | tf_op jit(solution)/shard_map/jit(cholesky)/cholesky | solution.py:35
  546.2 11.7 %cholesky.238 = f32[128,128]{1,0:T(8,128)S(1)} custom-call(f32[128,128]{1,0:T(8,128)S(1)} %cholesky.275), custom_call_target="Cholesky" | custom-call | tf_op jit(solution)/shard_map/jit(cholesky)/cholesky | solution.py:35
  558.6 9.8 %custom-call.32 = f32[1,128,128]{1,2,0:T(8,128)S(1)} custom-call(f32[1,128,128]{2,1,0:T(8,128)S(1)} %get-tuple-element.31), custom_call_target="InvertDiagBlocksLowerTriangular" | custom-call | tf_op jit(solution)/shard_map/jit(cholesky)/cholesky | solution.py:35
  569.9 11.9 %cholesky.255 = f32[128,128]{1,0:T(8,128)S(1)} custom-call(f32[128,128]{1,0:T(8,128)S(1)} %convolution_subtract_fusion.5), custom_call_target="Cholesky" | custom-call | tf_op jit(solution)/shard_map/jit(cholesky)/cholesky | solution.py:35
  586.9 11.7 %while.1 = (s32[]{:T(128)}, f32[512,512]{1,0:T(8,128)}, s32[4,2]{0,1:T(2,128)S(1)}, f32[4,128,128]{2,1,0:T(8,128)S(1)}, s32[]{:T(128)}) while((s32[]{:T(128)}, f32[512,512]{1,0:T(8,128)}, s32[4,2]{0,1:T(2,128)S(1)}, f32[4,128,128]{2,1,0:T(8,128)S(1)}, s32[]{:T(128)}) %tuple.33), condition=%wide.while_cond, body=%wide.while_body.sunk | while | flops 2 | bytes 131181 | solution.py:36
  587.6 2.2 bitcast_dynamic-update-slice_fusion.2
  590.5 2.2 bitcast_dynamic-update-slice_fusion.2
  593.5 2.2 bitcast_dynamic-update-slice_fusion.2
  596.4 2.2 bitcast_dynamic-update-slice_fusion.2
  598.6 39.3 %custom-call.33 = f32[4,128,128]{1,2,0:T(8,128)S(1)} custom-call(f32[4,128,128]{2,1,0:T(8,128)S(1)} %get-tuple-element.9), custom_call_target="InvertDiagBlocksLowerTriangular" | custom-call | tf_op jit(solution)/shard_map/triangular_solve | solution.py:36
  639.8 1.5 convolution_subtract_fusion.2
  641.6 1.8 convolution_subtract_fusion.1
  (55 shorter events, 17.9 us)
Async XLA Ops:
  7.2 237.1 %all-reduce.11.cloned.1.call-start = ((), (), s32[]{:S(2)}) async-start(), calls=%async_computation.2 | async-start | bytes 12582912 | tf_op jit(solution)/shard_map/psum | solution.py:30
  7.9 7.4 %copy-start = (f32[256,1024]{1,0:T(8,128)S(1)}, f32[256,1024]{1,0:T(8,128)}, u32[]{:S(2)}) copy-start(f32[256,1024]{1,0:T(8,128)} %param.3) | copy-start | bytes 3145732
  7.9 7.3 %copy-start.4 = (f32[256,512]{1,0:T(8,128)S(1)}, f32[256,512]{1,0:T(8,128)}, u32[]{:S(2)}) copy-start(f32[256,512]{1,0:T(8,128)} %param.4) | copy-start | bytes 1572868
  18.5 332.0 %all-reduce.9.cloned.1.call-start = ((), (), s32[]{:S(2)}) async-start(), calls=%async_computation.1 | async-start | bytes 12582912 | tf_op jit(solution)/shard_map/psum | solution.py:30
  244.3 251.5 %all-reduce.7.cloned.1.call-start = ((), (), s32[]{:S(2)}) async-start(), calls=%async_computation | async-start | bytes 2097152 | tf_op jit(solution)/shard_map/psum | solution.py:34
  350.5 10.1 %copy-start.1 = (f32[1024,512]{1,0:T(8,128)S(1)}, f32[1024,512]{1,0:T(8,128)}, u32[]{:S(2)}) copy-start(f32[1024,512]{1,0:T(8,128)} %get-tuple-element.20) | copy-start | bytes 6291460
  495.8 1.7 copy-start.2
  497.7 1.0 copy-start.3
Sparse Core Ops, SparseCore 0:
  18.7 225.5 all-reduce.10
  247.6 102.8 all-reduce.8
  364.9 130.8 all-reduce.6

commit v2 on v0

--- a/solution.py
+++ b/solution.py
@@ -31,7 +31,7 @@
     correction = coeffs - matrix_product(metric, coeffs)
     residual = block_live - matrix_product(basis_live, coeffs + correction)
     local_gram = transposed_product(residual, residual) * weight
-    gram = lax.psum(local_gram, ("grp", "row"))
+    gram = lax.psum(lax.psum(local_gram, "row"), "grp")
     lower_factor = jnp.linalg.cholesky(gram)
     new_block = lax.linalg.triangular_solve(
         lower_factor, residual, left_side=False, lower=True, transpose_a=True

time: 487 us -> 464 us (0.953)
  waiting for transfers between devices: 290 us -> 269 us
    psum x1 -> x2, waiting for transfers between devices: 131 us -> 110 us  [body(): gram = lax.psum(lax.psum(local_gram, 'row'), 'grp')]
  transfers between devices with their start and end apart: 2 -> 3, of which waited for: 2 -> 3; matrix products, arithmetic and copies ran while one was open for 0% -> 0% of each run, Pallas kernels for 0% -> 0%
where the time goes in v2:
time: 464 us; the launch traced here: 459 us
  waiting for transfers between devices  269 us (58%)
  other arithmetic  120 us (26%)
  matrix products  35.6 us (8%)
  between operations  17.5 us (4%)
  local copies, waits for them, and re-layouts  16.7 us (4%)
    psum x1, waiting for transfers between devices, body(): coeffs, metric = lax.psum((local_coeffs, local_metric), ('grp', 'row'))  159 us
    psum x2, waiting for transfers between devices, body(): gram = lax.psum(lax.psum(local_gram, 'row'), 'grp')  110 us
    another operation x14, other arithmetic, body(): lower_factor = jnp.linalg.cholesky(gram)  78.6 us
    another operation x3, other arithmetic, body(): lax.linalg.triangular_solve(lower_factor, residual, left_side=False, lowe...  39.4 us
    dot_general x3, matrix products, transposed_product(): lax.dot_general(left, right, (((0,), (0,)), ((), ())), precision=lax.Prec...  12.6 us
    dot_general x2, matrix products, matrix_product(): jnp.dot(left, right, precision=lax.Precision.HIGHEST, preferred_element_t...  11.7 us
    another operation x12, local copies, waits for them, and re-layouts  11.6 us
  transfers between devices with their start and end apart: 3, of which 3 were waited for; matrix products, arithmetic and copies ran while one was open for 0% of the time, Pallas kernels for 0%

profile of v2, /device:TPU:0, one launch (start us, length us, event | category | flops | bytes accessed | tf_op | source)
XLA Modules:
  0.0 458.8 jit_solution(1911514309770503720)
XLA Ops:
  7.9 7.3 %convolution_multiply_fusion = f32[1024,1024]{1,0:T(8,128)} fusion(f32[256,1024]{1,0:T(8,128)} %param.3, f32[256]{0:T(256)S(1)} %compare_convert_fusion), kind=kOutput, calls=%fused_computation.3 | convolution fusion | flops 3222536192 | bytes 5243904 | tf_op jit(solution)/shard_map/dot_general | solution.py:8
  15.2 3.3 convolution_multiply_fusion.1
  19.1 158.5 %all-reduce.10.cloned.1.call-done = (f32[1024,512]{1,0:T(8,128)}, f32[1024,1024]{1,0:T(8,128)}) async-done(((f32[1024,512]{1,0:T(8,128)}, f32[1024,1024]{1,0:T(8,128)}), (f32[1024,512]{1,0:T(8,128)}, f32[1024,1024]{1,0:T(8,128)})) %all-reduce.10.cloned.1.call-update) | async-done | bytes 6291472 | tf_op jit(solution)/shard_map/psum | solution.py:30
  177.6 9.6 %fusion.43 = f32[1024,512]{1,0:T(8,128)S(1)} fusion(f32[1024,1024]{1,0:T(8,128)} %get-tuple-element.21, f32[1024,512]{1,0:T(8,128)} %get-tuple-element.20), kind=kOutput, calls=%fused_computation.84 | convolution fusion | flops 6442450944 | bytes 8388608 | tf_op jit(solution)/shard_map/dot_general | solution.py:18
  187.3 2.1 fusion.1
  189.4 2.0 convolution_multiply_fusion.2
  191.7 56.4 %all-reduce.6.cloned.1.call-done = f32[512,512]{0,1:T(8,128)} async-done(((f32[512,512]{0,1:T(8,128)}), f32[512,512]{0,1:T(8,128)}) %all-reduce.6.cloned.1.call-update) | async-done | bytes 1048592 | tf_op jit(solution)/shard_map/psum | solution.py:34
  248.1 53.5 %all-reduce.8.cloned.1.call-done = f32[512,512]{0,1:T(8,128)} async-done(((f32[512,512]{0,1:T(8,128)}), f32[512,512]{0,1:T(8,128)}) %all-reduce.8.cloned.1.call-update) | async-done | bytes 1048592 | tf_op jit(solution)/shard_map/psum | solution.py:34
  301.6 1.6 copy.6
  304.5 11.7 %cholesky.104 = f32[128,128]{1,0:T(8,128)S(1)} custom-call(f32[128,128]{1,0:T(8,128)S(1)} %cholesky.266), custom_call_target="Cholesky" | custom-call | tf_op jit(solution)/shard_map/jit(cholesky)/cholesky | solution.py:35
  316.3 9.8 %custom-call.30 = f32[1,128,128]{1,2,0:T(8,128)S(1)} custom-call(f32[1,128,128]{2,1,0:T(8,128)S(1)} %get-tuple-element.35), custom_call_target="InvertDiagBlocksLowerTriangular" | custom-call | tf_op jit(solution)/shard_map/jit(cholesky)/cholesky | solution.py:35
  328.7 11.7 %cholesky.217 = f32[128,128]{1,0:T(8,128)S(1)} custom-call(f32[128,128]{1,0:T(8,128)S(1)} %cholesky.270), custom_call_target="Cholesky" | custom-call | tf_op jit(solution)/shard_map/jit(cholesky)/cholesky | solution.py:35
  340.5 10.0 %custom-call.31 = f32[1,128,128]{1,2,0:T(8,128)S(1)} custom-call(f32[1,128,128]{2,1,0:T(8,128)S(1)} %get-tuple-element.32), custom_call_target="InvertDiagBlocksLowerTriangular" | custom-call | tf_op jit(solution)/shard_map/jit(cholesky)/cholesky | solution.py:35
  352.0 11.7 %cholesky.238 = f32[128,128]{1,0:T(8,128)S(1)} custom-call(f32[128,128]{1,0:T(8,128)S(1)} %cholesky.275), custom_call_target="Cholesky" | custom-call | tf_op jit(solution)/shard_map/jit(cholesky)/cholesky | solution.py:35
  364.5 9.8 %custom-call.32 = f32[1,128,128]{1,2,0:T(8,128)S(1)} custom-call(f32[1,128,128]{2,1,0:T(8,128)S(1)} %get-tuple-element.29), custom_call_target="InvertDiagBlocksLowerTriangular" | custom-call | tf_op jit(solution)/shard_map/jit(cholesky)/cholesky | solution.py:35
  375.8 11.7 %cholesky.255 = f32[128,128]{1,0:T(8,128)S(1)} custom-call(f32[128,128]{1,0:T(8,128)S(1)} %convolution_subtract_fusion.5), custom_call_target="Cholesky" | custom-call | tf_op jit(solution)/shard_map/jit(cholesky)/cholesky | solution.py:35
  392.8 11.7 %while.1 = (s32[]{:T(128)}, f32[512,512]{1,0:T(8,128)}, s32[4,2]{0,1:T(2,128)S(1)}, f32[4,128,128]{2,1,0:T(8,128)S(1)}, s32[]{:T(128)}) while((s32[]{:T(128)}, f32[512,512]{1,0:T(8,128)}, s32[4,2]{0,1:T(2,128)S(1)}, f32[4,128,128]{2,1,0:T(8,128)S(1)}, s32[]{:T(128)}) %tuple.33), condition=%wide.while_cond, body=%wide.while_body.sunk | while | flops 2 | bytes 131181 | solution.py:36
  393.5 2.2 bitcast_dynamic-update-slice_fusion.2
  396.5 2.2 bitcast_dynamic-update-slice_fusion.2
  399.4 2.2 bitcast_dynamic-update-slice_fusion.2
  402.3 2.2 bitcast_dynamic-update-slice_fusion.2
  404.5 39.3 %custom-call.33 = f32[4,128,128]{1,2,0:T(8,128)S(1)} custom-call(f32[4,128,128]{2,1,0:T(8,128)S(1)} %get-tuple-element.9), custom_call_target="InvertDiagBlocksLowerTriangular" | custom-call | tf_op jit(solution)/shard_map/triangular_solve | solution.py:36
  445.7 1.5 convolution_subtract_fusion.2
  447.6 1.8 convolution_subtract_fusion.1
  (55 shorter events, 18.9 us)
Async XLA Ops:
  7.2 170.5 %all-reduce.10.cloned.1.call-start = ((), (), s32[]{:S(2)}) async-start(), calls=%async_computation.2 | async-start | bytes 12582912 | tf_op jit(solution)/shard_map/psum | solution.py:30
  7.9 7.4 %copy-start = (f32[256,1024]{1,0:T(8,128)S(1)}, f32[256,1024]{1,0:T(8,128)}, u32[]{:S(2)}) copy-start(f32[256,1024]{1,0:T(8,128)} %param.3) | copy-start | bytes 3145732
  7.9 7.3 %copy-start.4 = (f32[256,512]{1,0:T(8,128)S(1)}, f32[256,512]{1,0:T(8,128)}, u32[]{:S(2)}) copy-start(f32[256,512]{1,0:T(8,128)} %param.4) | copy-start | bytes 1572868
  18.5 229.6 %all-reduce.6.cloned.1.call-start = ((), (), s32[]{:S(2)}) async-start(), calls=%async_computation | async-start | bytes 2097152 | tf_op jit(solution)/shard_map/psum | solution.py:34
  177.6 9.6 %copy-start.1 = (f32[1024,512]{1,0:T(8,128)S(1)}, f32[1024,512]{1,0:T(8,128)}, u32[]{:S(2)}) copy-start(f32[1024,512]{1,0:T(8,128)} %get-tuple-element.20) | copy-start | bytes 6291460
  191.4 110.2 %all-reduce.8.cloned.1.call-start = ((), (), s32[]{:S(2)}) async-start(), calls=%async_computation.1 | async-start | bytes 2097152 | tf_op jit(solution)/shard_map/psum | solution.py:34
  301.6 1.7 copy-start.2
  303.5 1.0 copy-start.3
Sparse Core Ops, SparseCore 0:
  18.7 158.9 all-reduce.9
  191.6 56.4 all-reduce.5
  250.5 51.1 all-reduce.7
